TPU v7x, 32 devices: a whole 2x2x4 slice. The times are simulated.
32 devices in a mesh: dp: 8 (over y, x, core), rep: 4 (over z).
Axes of the slice: x: 2, y: 2, z: 4, core: 2. Of those that a mesh axis runs over, the one named last changes fastest.
Arguments:
- inputs: bfloat16 [32, 1044, 512], P(('dp', 'rep')), may hold values from -6 to 6
- segments: int32 [32, 1024], P(('dp', 'rep')), may hold values from 0 to 3, never falling along the last dimension, each value on 1 to 512 neighbouring positions
- cotangent: bfloat16 [32, 1044, 512], P(('dp', 'rep')), may hold values from -6 to 6
- attend_in: float32 [512, 1536], P(('dp', 'rep'))
- attend_out: float32 [512, 512], P(('dp', 'rep'))
- expand: float32 [512, 2048], P(('dp', 'rep'))
- contract: float32 [2048, 512], P(('dp', 'rep'))
- layer_norms: float32 [4, 512], P(None, ('dp', 'rep'))
- moment_in: float32 [512, 1536], P(('dp', 'rep')), may hold values from -512 to 512
- moment_out: float32 [512, 512], P(('dp', 'rep')), may hold values from -112 to 112
- moment_expand: float32 [512, 2048], P(('dp', 'rep')), may hold values from -320 to 320
- moment_contract: float32 [2048, 512], P(('dp', 'rep')), may hold values from -640 to 640
- moment_norms: float32 [4, 512], P(None, ('dp', 'rep')), may hold values from -1024 to 1024
- square_in: float32 [512, 1536], P(('dp', 'rep')), may hold values from 8352 to 33408
- square_out: float32 [512, 512], P(('dp', 'rep')), may hold values from 334 to 1336
- square_expand: float32 [512, 2048], P(('dp', 'rep')), may hold values from 3037 to 12148
- square_contract: float32 [2048, 512], P(('dp', 'rep')), may hold values from 12026 to 48107
- square_norms: float32 [4, 512], P(None, ('dp', 'rep')), may hold values from 33408 to 133632
Outputs:
- outputs: bfloat16 [32, 1044, 512], P(('dp', 'rep'))
- input_gradient: bfloat16 [32, 1044, 512], P(('dp', 'rep'))
- updated_in: float32 [512, 1536], P(('dp', 'rep'))
- updated_out: float32 [512, 512], P(('dp', 'rep'))
- updated_expand: float32 [512, 2048], P(('dp', 'rep'))
- updated_contract: float32 [2048, 512], P(('dp', 'rep'))
- updated_norms: float32 [4, 512], P(None, ('dp', 'rep'))
- momentum_in: float32 [512, 1536], P(('dp', 'rep'))
- momentum_out: float32 [512, 512], P(('dp', 'rep'))
- momentum_expand: float32 [512, 2048], P(('dp', 'rep'))
- momentum_contract: float32 [2048, 512], P(('dp', 'rep'))
- momentum_norms: float32 [4, 512], P(None, ('dp', 'rep'))
- variance_in: float32 [512, 1536], P(('dp', 'rep'))
- variance_out: float32 [512, 512], P(('dp', 'rep'))
- variance_expand: float32 [512, 2048], P(('dp', 'rep'))
- variance_contract: float32 [2048, 512], P(('dp', 'rep'))
- variance_norms: float32 [4, 512], P(None, ('dp', 'rep'))
- trust_table: float32 [3, 5], replicated
Inputs may be any that keep to these rules, and one draw needn't show every extreme that they name: `segments`: along a row the ids never fall; every id occurs, a segment holds at most 512 positions and in every row one holds exactly that many.
All inputs are finite; a program needn't handle non-finite values.
Results may differ from a plain program's by a relative error of at most 0.019.
The roundings to bfloat16 on the way count: a program that leaves them out, or rounds other values in their place, can miss the bound.
Values may be sent and summed in bfloat16 or wider, within the bound.
No kernel may reach another device: no remote copies, remote signals or barrier semaphores. Data moves between devices by JAX's collectives and lax.ppermute only.
A program may use at most 128 MiB of HBM per device.

v0:
```python
from functools import partial
import math

import jax
import jax.numpy as jnp
from jax import lax
from jax.sharding import PartitionSpec as P

HEADS = 8
HEAD_DIM = 64


EPSILON = 1e-05
ADAM_EPSILON = 1e-06
DECAY = 0.01
RATE = 0.5
BETA = 0.5
NEGATIVE = -1e30


def layer_norm(values, gain, bias):
    center = values - jnp.mean(values, axis=-1, keepdims=True)
    scale = lax.rsqrt(jnp.mean(center * center, axis=-1, keepdims=True) + EPSILON)
    normed = center * scale
    return (normed * gain + bias, normed, scale)


def norm_backward(grad_out, normed, scale, gain):
    scaled = grad_out * gain
    grad_in = scale * (
        scaled
        - jnp.mean(scaled, axis=-1, keepdims=True)
        - normed * jnp.mean(scaled * normed, axis=-1, keepdims=True)
    )
    return (grad_in, jnp.sum(grad_out * normed, axis=0), jnp.sum(grad_out, axis=0))


def allowed_mask(segment_row, rows):
    memory = rows - segment_row.shape[0]
    labels = jnp.concatenate([jnp.full((memory,), -1, jnp.int32), segment_row])
    return (labels[:, None] == labels[None, :]) | (labels[:, None] < 0) | (labels[None, :] < 0)


def head_scores(queries, keys, allowed):
    scores = jnp.einsum("qd,kd->qk", queries, keys, preferred_element_type=jnp.float32)
    return jnp.where(allowed, scores * (1.0 / math.sqrt(HEAD_DIM)), NEGATIVE)


def forward_sequence(weights, values_in, segment_row):
    attend_in, attend_out, expand, contract, norms = weights
    gains = norms.astype(jnp.float32)
    rows = values_in.shape[0]
    allowed = allowed_mask(segment_row, rows)
    start = values_in.astype(jnp.float32)
    first_norm, normed_one, scale_one = layer_norm(start, gains[0], gains[1])
    first_low = first_norm.astype(jnp.bfloat16)
    packed = jnp.dot(first_low, attend_in, preferred_element_type=jnp.float32).astype(jnp.bfloat16)
    parts = packed.reshape(rows, 3, HEADS, HEAD_DIM).transpose(1, 2, 0, 3)

    def one_head(triple):
        queries, keys, values = triple
        scores = head_scores(queries, keys, allowed)
        highest = jnp.max(scores, axis=-1, keepdims=True)
        raised = jnp.exp(scores - highest)
        total = jnp.sum(raised, axis=-1, keepdims=True)
        attention = (raised / total).astype(jnp.bfloat16)
        return (
            jnp.dot(attention, values, preferred_element_type=jnp.float32),
            highest + jnp.log(total),
        )

    mixed_heads, log_totals = lax.map(one_head, (parts[0], parts[1], parts[2]))
    mixed = mixed_heads.transpose(1, 0, 2).reshape(rows, -1).astype(jnp.bfloat16)
    middle = start + jnp.dot(mixed, attend_out, preferred_element_type=jnp.float32)
    second_norm, normed_two, scale_two = layer_norm(middle, gains[2], gains[3])
    second_low = second_norm.astype(jnp.bfloat16)
    hidden = jnp.dot(second_low, expand, preferred_element_type=jnp.float32)
    active = jax.nn.gelu(hidden, approximate=True).astype(jnp.bfloat16)
    result = middle + jnp.dot(active, contract, preferred_element_type=jnp.float32)
    saved = (
        allowed,
        gains,
        normed_one,
        scale_one,
        first_low,
        parts,
        log_totals,
        mixed,
        normed_two,
        scale_two,
        second_low,
        hidden,
        active,
    )
    return (result, saved)


def backward_sequence(weights, values_in, segment_row, cotangent):
    attend_in, attend_out, expand, contract, norms = weights
    result, saved = forward_sequence(weights, values_in, segment_row)
    (
        allowed,
        gains,
        normed_one,
        scale_one,
        first_low,
        parts,
        log_totals,
        mixed,
        normed_two,
        scale_two,
        second_low,
        hidden,
        active,
    ) = saved
    rows = values_in.shape[0]
    grad_out = cotangent.astype(jnp.float32)
    grad_low = grad_out.astype(jnp.bfloat16)
    grad_contract = jnp.einsum("rf,rd->fd", active, grad_low, preferred_element_type=jnp.float32)
    grad_active = jnp.einsum("rd,fd->rf", grad_low, contract, preferred_element_type=jnp.float32)
    gelu_value, gelu_back = jax.vjp(partial(jax.nn.gelu, approximate=True), hidden)
    grad_hidden = gelu_back(grad_active)[0].astype(jnp.bfloat16)
    grad_expand = jnp.einsum(
        "rd,rf->df", second_low, grad_hidden, preferred_element_type=jnp.float32
    )
    grad_second = jnp.einsum("rf,df->rd", grad_hidden, expand, preferred_element_type=jnp.float32)
    back_two, gain_two, bias_two = norm_backward(grad_second, normed_two, scale_two, gains[2])
    grad_middle = grad_out + back_two
    middle_low = grad_middle.astype(jnp.bfloat16)
    grad_attend_out = jnp.einsum("rd,re->de", mixed, middle_low, preferred_element_type=jnp.float32)
    grad_mixed = jnp.einsum(
        "re,de->rd", middle_low, attend_out, preferred_element_type=jnp.float32
    ).astype(jnp.bfloat16)
    upstream_heads = grad_mixed.reshape(rows, HEADS, HEAD_DIM).transpose(1, 0, 2)
    factor = 1.0 / math.sqrt(HEAD_DIM)

    def head_back(items):
        queries, keys, values, upstream, log_total = items
        scores = head_scores(queries, keys, allowed)
        attention = jnp.exp(scores - log_total)
        grad_attention = jnp.einsum(
            "qd,kd->qk", upstream, values, preferred_element_type=jnp.float32
        )
        inner = jnp.sum(attention * grad_attention, axis=-1, keepdims=True)
        grad_scores = (attention * (grad_attention - inner)).astype(jnp.bfloat16)
        grad_queries = jnp.dot(grad_scores, keys, preferred_element_type=jnp.float32) * factor
        grad_keys = (
            jnp.einsum("qk,qd->kd", grad_scores, queries, preferred_element_type=jnp.float32)
            * factor
        )
        grad_values = jnp.einsum(
            "qk,qd->kd",
            attention.astype(jnp.bfloat16),
            upstream,
            preferred_element_type=jnp.float32,
        )
        return jnp.stack([grad_queries, grad_keys, grad_values])

    head_grads = lax.map(head_back, (parts[0], parts[1], parts[2], upstream_heads, log_totals))
    grad_packed = head_grads.transpose(2, 1, 0, 3).reshape(rows, -1).astype(jnp.bfloat16)
    grad_attend_in = jnp.einsum(
        "rd,re->de", first_low, grad_packed, preferred_element_type=jnp.float32
    )
    grad_first = jnp.einsum("re,de->rd", grad_packed, attend_in, preferred_element_type=jnp.float32)
    back_one, gain_one, bias_one = norm_backward(grad_first, normed_one, scale_one, gains[0])
    grad_input = (grad_middle + back_one).astype(jnp.bfloat16)
    grad_norms = jnp.stack([gain_one, bias_one, gain_two, bias_two])
    return (grad_input, (grad_attend_in, grad_attend_out, grad_expand, grad_contract, grad_norms))


def body(
    inputs,
    segments,
    cotangent,
    attend_in,
    attend_out,
    expand,
    contract,
    layer_norms,
    moment_in,
    moment_out,
    moment_expand,
    moment_contract,
    moment_norms,
    square_in,
    square_out,
    square_expand,
    square_contract,
    square_norms,
):
    masters = (attend_in, attend_out, expand, contract, layer_norms)
    local_weight_sums = jnp.stack([jnp.sum(weight * weight) for weight in masters])
    lowered = [weight.astype(jnp.bfloat16) for weight in masters]
    gathered = (
        lax.all_gather(lowered[0], ("dp", "rep"), axis=0, tiled=True),
        lax.all_gather(lowered[1], ("dp", "rep"), axis=0, tiled=True),
        lax.all_gather(lowered[2], ("dp", "rep"), axis=0, tiled=True),
        lax.all_gather(lowered[3], ("dp", "rep"), axis=0, tiled=True),
        lax.all_gather(lowered[4], ("dp", "rep"), axis=1, tiled=True),
    )

    def forward_one(items):
        return forward_sequence(gathered, items[0], items[1])[0].astype(jnp.bfloat16)

    outputs = lax.map(forward_one, (inputs, segments))
    regathered = (
        lax.all_gather(lowered[0], ("dp", "rep"), axis=0, tiled=True),
        lax.all_gather(lowered[1], ("dp", "rep"), axis=0, tiled=True),
        lax.all_gather(lowered[2], ("dp", "rep"), axis=0, tiled=True),
        lax.all_gather(lowered[3], ("dp", "rep"), axis=0, tiled=True),
        lax.all_gather(lowered[4], ("dp", "rep"), axis=1, tiled=True),
    )
    zero_grads = tuple((jnp.zeros(weight.shape, jnp.float32) for weight in regathered))

    def accumulate(carry, items):
        grad_input, grads = backward_sequence(regathered, items[0], items[1], items[2])
        return (tuple((total + piece for total, piece in zip(carry, grads))), grad_input)

    summed, input_gradient = lax.scan(accumulate, zero_grads, (inputs, segments, cotangent))
    reduced = (
        lax.psum_scatter(summed[0], ("dp", "rep"), scatter_dimension=0, tiled=True),
        lax.psum_scatter(summed[1], ("dp", "rep"), scatter_dimension=0, tiled=True),
        lax.psum_scatter(summed[2], ("dp", "rep"), scatter_dimension=0, tiled=True),
        lax.psum_scatter(summed[3], ("dp", "rep"), scatter_dimension=0, tiled=True),
        lax.psum_scatter(summed[4], ("dp", "rep"), scatter_dimension=1, tiled=True),
    )
    firsts = (moment_in, moment_out, moment_expand, moment_contract, moment_norms)
    seconds = (square_in, square_out, square_expand, square_contract, square_norms)
    momenta = []
    variances = []
    directions = []
    for weight, gradient, first, second in zip(masters, reduced, firsts, seconds):
        momentum = BETA * first + (1.0 - BETA) * gradient
        variance = BETA * second + (1.0 - BETA) * gradient * gradient
        momenta.append(momentum)
        variances.append(variance)
        directions.append(momentum / (jnp.sqrt(variance) + ADAM_EPSILON) + DECAY * weight)
    local_update_sums = jnp.stack([jnp.sum(direction * direction) for direction in directions])
    weight_sums, update_sums = lax.psum((local_weight_sums, local_update_sums), ("dp", "rep"))
    weight_norms = jnp.sqrt(weight_sums)
    update_norms = jnp.sqrt(update_sums)
    ratios = weight_norms / update_norms
    updated = [
        weight - RATE * ratios[index] * direction
        for index, (weight, direction) in enumerate(zip(masters, directions))
    ]
    trust_table = jnp.stack([weight_norms, update_norms, ratios])
    return (
        outputs,
        input_gradient,
        updated[0],
        updated[1],
        updated[2],
        updated[3],
        updated[4],
        momenta[0],
        momenta[1],
        momenta[2],
        momenta[3],
        momenta[4],
        variances[0],
        variances[1],
        variances[2],
        variances[3],
        variances[4],
        trust_table,
    )


def solution(mesh):
    placed = (
        P(("dp", "rep"), None, None),
        P(("dp", "rep"), None),
        P(("dp", "rep"), None, None),
        P(("dp", "rep"), None),
        P(("dp", "rep"), None),
        P(("dp", "rep"), None),
        P(("dp", "rep"), None),
        P(None, ("dp", "rep")),
        P(("dp", "rep"), None),
        P(("dp", "rep"), None),
        P(("dp", "rep"), None),
        P(("dp", "rep"), None),
        P(None, ("dp", "rep")),
        P(("dp", "rep"), None),
        P(("dp", "rep"), None),
        P(("dp", "rep"), None),
        P(("dp", "rep"), None),
        P(None, ("dp", "rep")),
    )
    return jax.shard_map(
        body,
        mesh=mesh,
        in_specs=placed,
        out_specs=(
            P(("dp", "rep"), None, None),
            P(("dp", "rep"), None, None),
            P(("dp", "rep"), None),
            P(("dp", "rep"), None),
            P(("dp", "rep"), None),
            P(("dp", "rep"), None),
            P(None, ("dp", "rep")),
            P(("dp", "rep"), None),
            P(("dp", "rep"), None),
            P(("dp", "rep"), None),
            P(("dp", "rep"), None),
            P(None, ("dp", "rep")),
            P(("dp", "rep"), None),
            P(("dp", "rep"), None),
            P(("dp", "rep"), None),
            P(("dp", "rep"), None),
            P(None, ("dp", "rep")),
            P(),
        ),
        check_vma=False,
    )
```

profile of v0, /device:TPU:0, one launch (start us, length us, event | category | flops | bytes accessed | tf_op | source)
XLA Modules:
  0.0 1165.1 jit_solution(12380102914019008058)
XLA Ops:
  11.9 69.8 %all-gather = bf16[32,16,4]{1,2,0:T(4,128)(2,1)S(1)} all-gather(bf16[1,16,4]{1,2,0:T(4,128)(2,1)S(1)} %get-tuple-element.431), channel_id=1, replica_groups=mesh['dp'=8,'rep'=4] {'dp','rep'}, dimensions={0}, use_global_device_ids=true | all-gather | bytes 4224 | tf_op jit(solution)/shard_map/all_gather | solution.py:199
  84.3 73.8 %all_gather.22 = bf16[512,512]{1,0:T(8,128)(2,1)} all-gather(bf16[16,512]{1,0:T(8,128)(2,1)S(1)} %convert_element_type.144), channel_id=1, replica_groups=mesh['dp'=8,'rep'=4] {'dp','rep'}, dimensions={0}, use_global_device_ids=true | all-gather | bytes 540672 | tf_op jit(solution)/shard_map/all_gather | solution.py:196
  158.2 5.1 convolution_convert_fusion
  163.3 5.4 copy.68
  168.7 3.3 slice_bitcast_fusion
  172.0 3.7 copy.69
  180.5 47.1 %while.59 = (s32[]{:T(128)}, bf16[8,1044,64]{1,2,0:T(8,128)(2,1)S(1)}, f32[8,1044,1]{1,2,0:T(1,128)}, bf16[8,1044,64]{2,1,0:T(8,128)(2,1)}, bf16[8,1044,64]{2,1,...) while((s32[]{:T(128)}, ...), condition=%wide.region_11.12_spmd.clone, body=%wide.region_8.11_spmd.clone.sunk | while | flops 291011872 | bytes 14721805 | solution.py:72
  231.4 4.2 fusion.141
  235.6 3.3 copy-done.32
  238.9 5.2 fusion.78
  244.2 145.4 %reduce-scatter.14.cloned.1.call-done = f32[64,512]{1,0:T(8,128)} async-done(((f32[2048,512]{1,0:T(8,128)}), f32[64,512]{1,0:T(8,128)}) %reduce-scatter.14.cloned.1.call-update) | async-done | bytes 131088 | tf_op jit(solution)/shard_map/reduce_scatter | solution.py:224
  392.3 55.7 %all-gather.9.cloned.1.call-done = bf16[2048,512]{1,0:T(8,128)(2,1)} async-done(((bf16[64,512]{1,0:T(8,128)(2,1)}), bf16[2048,512]{1,0:T(8,128)(2,1)}) %all-gather.9.cloned.1.call-update) | async-done | bytes 2097168 | tf_op jit(solution)/shard_map/all_gather | solution.py:198
  448.0 9.9 fusion.69
  467.5 99.7 %while.60 = (s32[]{:T(128)}, bf16[8,3,1044,64]{2,3,1,0:T(8,128)(2,1)}, bf16[8,1044,64]{2,1,0:T(8,128)(2,1)}, bf16[8,1044,64]{2,1,0:T(8,128)(2,1)}, f32[8,1044,1]...) while((s32[]{:T(128)}, ...), condition=%wide.region_18.19_spmd.clone, body=%wide.region_16.18_spmd.clone.sunk | while | flops 712107200 | bytes 36097608 | solution.py:159
  470.3 3.2 multiply_reduce_fusion.18
  482.8 3.2 multiply_reduce_fusion.18
  532.5 3.2 multiply_reduce_fusion.18
  545.0 3.2 multiply_reduce_fusion.18
  569.8 4.0 fusion.95
  574.7 3.8 fusion.124
  578.6 6.5 fusion.102
  585.2 7.3 fusion.140
  592.6 42.3 %while.58 = (s32[]{:T(128)}, bf16[8,1044,64]{1,2,0:T(8,128)(2,1)S(1)}, bf16[8,1044,64]{2,1,0:T(8,128)(2,1)}, bf16[8,1044,64]{2,1,0:T(8,128)(2,1)}, bf16[8,1044,6...) while((s32[]{:T(128)}, ...), condition=%wide.region_5.6_spmd.clone, body=%wide.region_2.5_spmd.clone.sunk | while | flops 291010816 | bytes 14699973 | solution.py:72
  637.8 9.6 fusion.81
  647.4 59.8 %reduce-scatter.16.cloned.1.call-done = f32[16,4]{1,0:T(8,128)} async-done(((f32[512,4]{1,0:T(8,128)}), f32[16,4]{1,0:T(8,128)}) %reduce-scatter.16.cloned.1.call-update) | async-done | bytes 272
  709.9 131.6 %reduce-scatter.10.cloned.1.call-done = f32[16,512]{1,0:T(8,128)} async-done(((f32[512,512]{1,0:T(8,128)}), f32[16,512]{1,0:T(8,128)}) %reduce-scatter.10.cloned.1.call-update) | async-done | bytes 32784 | tf_op jit(solution)/shard_map/reduce_scatter | solution.py:222
  843.6 101.6 %reduce-scatter.8.cloned.1.call-done = f32[16,1536]{1,0:T(8,128)} async-done(((f32[512,1536]{1,0:T(8,128)}), f32[16,1536]{1,0:T(8,128)}) %reduce-scatter.8.cloned.1.call-update) | async-done | bytes 98320 | tf_op jit(solution)/shard_map/reduce_scatter | solution.py:221
  947.5 147.3 %reduce-scatter.12.cloned.1.call-done = f32[16,2048]{1,0:T(8,128)} async-done(((f32[512,2048]{1,0:T(8,128)}), f32[16,2048]{1,0:T(8,128)}) %reduce-scatter.12.cloned.1.call-update) | async-done | bytes 131088 | tf_op jit(solution)/shard_map/reduce_scatter | solution.py:223
  1097.3 3.7 stack.85
  1101.0 3.7 stack.96
  1104.8 3.3 fusion.104
  1108.1 37.5 %all-reduce.1 = (f32[5]{0:T(128)S(1)}, f32[5]{0:T(128)S(1)}) all-reduce(f32[5]{0:T(128)} %stack.96, f32[5]{0:T(128)} %stack.85), channel_id=1, replica_groups=mesh['dp'=8,'rep'=4] {'dp','rep'}, use_global_device_ids=true, to_apply=%region_41.42 | all-reduce | flops 10 | bytes 80 | tf_op jit(solution)/shard_map/psum | solution.py:239
  (259 shorter events, 228.5 us)
Async XLA Ops:
  7.2 76.4 %copy-start.2 = (bf16[1,1044,512]{2,1,0:T(8,128)(2,1)S(1)}, bf16[1,1044,512]{2,1,0:T(8,128)(2,1)}, u32[]{:S(2)}) copy-start(bf16[1,1044,512]{2,1,0:T(8,128)(2,1)} %param.24) | copy-start | bytes 3207172
  7.2 77.0 %copy-start.24 = (s32[1,1024]{1,0:T(1,128)S(1)}, s32[1,1024]{1,0:T(1,128)}, u32[]{:S(2)}) copy-start(s32[1,1024]{1,0:T(1,128)} %param.25) | copy-start | bytes 12292
  7.2 77.1 %copy-start.15 = (f32[16,512]{1,0:T(8,128)S(1)}, f32[16,512]{1,0:T(8,128)}, u32[]{:S(2)}) copy-start(f32[16,512]{1,0:T(8,128)} %param.28) | copy-start | bytes 98308
  7.2 150.9 %all-gather.5.cloned.1.call-start = ((), (), s32[]{:S(2)}) async-start(), calls=%async_computation.5 | async-start | bytes 1622016 | tf_op jit(solution)/shard_map/all_gather | solution.py:195
  8.9 222.5 %all-gather.7.cloned.1.call-start = ((), (), s32[]{:S(2)}) async-start(), calls=%async_computation.6 | async-start | bytes 2162688 | tf_op jit(solution)/shard_map/all_gather | solution.py:197
  10.5 379.2 %reduce-scatter.14.cloned.1.call-start = ((), (), s32[]{:S(2)}) async-start(), calls=%async_computation.11 | async-start | bytes 4325376 | tf_op jit(solution)/shard_map/reduce_scatter | solution.py:224
  82.0 81.2 %copy-start.25 = (f32[1,512]{1,0:T(1,128)}, f32[1,512]{1,0:T(1,128)S(1)}, u32[]{:S(2)}) copy-start(f32[1,512]{1,0:T(1,128)S(1)} %get-tuple-element.429) | copy-start | bytes 6148
  82.1 81.2 %copy-start.28 = (f32[1,512]{1,0:T(1,128)}, f32[1,512]{1,0:T(1,128)S(1)}, u32[]{:S(2)}) copy-start(f32[1,512]{1,0:T(1,128)S(1)} %get-tuple-element.428) | copy-start | bytes 6148
  83.6 79.7 %copy-start.18 = (f32[1044]{0:T(1024)}, f32[1044]{0:T(1024)S(1)}, u32[]{:S(2)}) copy-start(f32[1044]{0:T(1024)S(1)} %broadcast_multiply_fusion.6) | copy-start | bytes 12532
  84.2 79.1 %copy-start.20 = (f32[1044]{0:T(1024)}, f32[1044]{0:T(1024)S(1)}, u32[]{:S(2)}) copy-start(f32[1044]{0:T(1024)S(1)} %add_rsqrt_fusion.2) | copy-start | bytes 12532
  231.4 7.5 copy-start.10
  235.6 3.3 copy-start.32
  244.2 145.5 %copy-start.13 = (f32[64,512]{1,0:T(8,128)S(1)}, f32[64,512]{1,0:T(8,128)}, u32[]{:S(2)}) copy-start(f32[64,512]{1,0:T(8,128)} %param.30) | copy-start | bytes 393220
  244.2 145.5 %copy-start.17 = (f32[64,512]{1,0:T(8,128)S(1)}, f32[64,512]{1,0:T(8,128)}, u32[]{:S(2)}) copy-start(f32[64,512]{1,0:T(8,128)} %param.40) | copy-start | bytes 393220
  244.2 203.9 %all-gather.9.cloned.1.call-start = ((), (), s32[]{:S(2)}) async-start(), calls=%async_computation.7 | async-start | bytes 2162688 | tf_op jit(solution)/shard_map/all_gather | solution.py:198
  392.1 315.1 %reduce-scatter.16.cloned.1.call-start = ((), (), s32[]{:S(2)}) async-start(), calls=%async_computation.12 | async-start | bytes 270336
  448.0 9.9 copy-start.30
  457.9 3.1 copy-start.11
  569.7 4.1 copy-start.8
  574.7 3.9 copy-start.29
  574.7 266.8 %reduce-scatter.10.cloned.1.call-start = ((), (), s32[]{:S(2)}) async-start(), calls=%async_computation.9 | async-start | bytes 1081344 | tf_op jit(solution)/shard_map/reduce_scatter | solution.py:222
  578.6 366.6 %reduce-scatter.8.cloned.1.call-start = ((), (), s32[]{:S(2)}) async-start(), calls=%async_computation.8 | async-start | bytes 3244032 | tf_op jit(solution)/shard_map/reduce_scatter | solution.py:221
  585.1 509.7 %reduce-scatter.12.cloned.1.call-start = ((), (), s32[]{:S(2)}) async-start(), calls=%async_computation.10 | async-start | bytes 4325376 | tf_op jit(solution)/shard_map/reduce_scatter | solution.py:223
  592.6 42.3 %copy-start.7 = (bf16[512,512]{1,0:T(8,128)(2,1)S(1)}, bf16[512,512]{1,0:T(8,128)(2,1)}, u32[]{:S(2)}) copy-start(bf16[512,512]{1,0:T(8,128)(2,1)} %all_gather.22) | copy-start | bytes 1572868
  637.7 70.3 %copy-start.23 = (f32[4,16]{1,0:T(4,128)S(1)}, f32[4,16]{1,0:T(4,128)}, u32[]{:S(2)}) copy-start(f32[4,16]{1,0:T(4,128)} %param.31) | copy-start | bytes 772
  637.7 70.3 %copy-start.27 = (f32[4,16]{1,0:T(4,128)S(1)}, f32[4,16]{1,0:T(4,128)}, u32[]{:S(2)}) copy-start(f32[4,16]{1,0:T(4,128)} %param.41) | copy-start | bytes 772
  637.7 203.8 %copy-start.16 = (f32[16,512]{1,0:T(8,128)S(1)}, f32[16,512]{1,0:T(8,128)}, u32[]{:S(2)}) copy-start(f32[16,512]{1,0:T(8,128)} %param.28) | copy-start | bytes 98308
  637.7 203.8 %copy-start.22 = (f32[16,512]{1,0:T(8,128)S(1)}, f32[16,512]{1,0:T(8,128)}, u32[]{:S(2)}) copy-start(f32[16,512]{1,0:T(8,128)} %param.38) | copy-start | bytes 98308
  637.7 307.4 %copy-start.12 = (f32[16,1536]{1,0:T(8,128)S(1)}, f32[16,1536]{1,0:T(8,128)}, u32[]{:S(2)}) copy-start(f32[16,1536]{1,0:T(8,128)} %param.27) | copy-start | bytes 294916
  637.8 457.0 %copy-start.9 = (f32[16,2048]{1,0:T(8,128)S(1)}, f32[16,2048]{1,0:T(8,128)}, u32[]{:S(2)}) copy-start(f32[16,2048]{1,0:T(8,128)} %param.29) | copy-start | bytes 393220
  637.8 467.0 %copy-start.1 = (f32[1044,512]{1,0:T(8,128)S(1)}, f32[1044,512]{1,0:T(8,128)}, u32[]{:S(2)}) copy-start(f32[1044,512]{1,0:T(8,128)} %copy-done) | copy-start | bytes 6414340
  947.5 208.7 %copy-start.14 = (f32[16,1536]{1,0:T(8,128)}, f32[16,1536]{1,0:T(8,128)S(1)}, u32[]{:S(2)}) copy-start(f32[16,1536]{1,0:T(8,128)S(1)} %get-tuple-element.414) | copy-start | bytes 294916
  (9 other events, 19.2 us)
Sparse Core Ops, SparseCore 0:
  11.5 57.7 all-gather.4
  72.8 55.8 all-gather.6
  244.3 145.3 reduce-scatter.13
  393.0 54.9 all-gather.8
  574.8 132.3 reduce-scatter.15
  710.0 131.4 reduce-scatter.9
  846.9 98.1 reduce-scatter.7
  947.4 147.3 reduce-scatter.11
where the time goes:
time: 1180 us; the launch traced here: 1170 us
  waiting for transfers between devices  642 us (54%)
  matrix products  218 us (18%)
  blocking collectives  181 us (15%)
  other arithmetic  56.3 us (5%)
  local copies, waits for them, and re-layouts  48.7 us (4%)
  between operations  18.3 us (2%)
    reduce_scatter x1, waiting for transfers between devices, body(): lax.psum_scatter(summed[2], ('dp', 'rep'), scatter_dimension=0, tiled=True)  147 us
    reduce_scatter x1, waiting for transfers between devices, body(): lax.psum_scatter(summed[3], ('dp', 'rep'), scatter_dimension=0, tiled=True)  145 us
    reduce_scatter x1, waiting for transfers between devices, body(): lax.psum_scatter(summed[1], ('dp', 'rep'), scatter_dimension=0, tiled=True)  132 us
    reduce_scatter x1, waiting for transfers between devices, body(): lax.psum_scatter(summed[0], ('dp', 'rep'), scatter_dimension=0, tiled=True)  102 us
    all_gather x1, blocking collectives, body(): lax.all_gather(lowered[1], ('dp', 'rep'), axis=0, tiled=True)  73.8 us
    all_gather x1, blocking collectives, body(): lax.all_gather(lowered[4], ('dp', 'rep'), axis=1, tiled=True)  69.8 us
    dot_general x24, matrix products, head_scores(): jnp.einsum('qd,kd->qk', queries, keys, preferred_element_type=jnp.float32)  67 us
    unnamed x9, waiting for transfers between devices  60 us
  transfers between devices with their start and end apart: 8, of which 6 were waited for; matrix products, arithmetic and copies ran while one was open for 13% of the time, Pallas kernels for 0%

commit v1 on v0

--- a/solution.py
+++ b/solution.py
@@ -165,10 +165,89 @@
     back_one, gain_one, bias_one = norm_backward(grad_first, normed_one, scale_one, gains[0])
     grad_input = (grad_middle + back_one).astype(jnp.bfloat16)
     grad_norms = jnp.stack([gain_one, bias_one, gain_two, bias_two])
-    return (grad_input, (grad_attend_in, grad_attend_out, grad_expand, grad_contract, grad_norms))
+    return (result, grad_input, (grad_attend_in, grad_attend_out, grad_expand, grad_contract, grad_norms))
+
+
+AXES = ("dp", "rep")
+
+
+class Layout:
+    def __init__(self, mesh):
+        self.dp = mesh.shape["dp"]
+        self.rep = mesh.shape["rep"]
+        self.plane = self.dp // 2
+
+    def permute(self, value, move):
+        pairs = []
+        for p in range(self.plane):
+            for c in range(2):
+                for z in range(self.rep):
+                    q, d, w = move(p, c, z)
+                    pairs.append(((p * 2 + c) * self.rep + z, (q * 2 + d) * self.rep + w))
+        return lax.ppermute(value, AXES, pairs)
+
+    def to_core(self, value):
+        return self.permute(value, lambda p, c, z: (p, 1 - c, z))
+
+    def to_plane(self, value, m):
+        return self.permute(value, lambda p, c, z: (p ^ m, c, z))
+
+    def to_rep(self, value, k):
+        return self.permute(value, lambda p, c, z: (p, c, (z + k) % self.rep))
+
+    def place(self):
+        dp = lax.axis_index("dp")
+        return dp // 2, dp % 2, lax.axis_index("rep")
+
+
+def pick(value, index, axis):
+    return lax.dynamic_index_in_dim(value, index, axis, keepdims=False)
+
+
+def gather_rows(lay, shard):
+    rows, cols = shard.shape
+    p, c, z = lay.place()
+    column = jnp.zeros((lay.rep, rows, cols), shard.dtype)
+    column = lax.dynamic_update_index_in_dim(column, shard, z, 0)
+    for k in range(1, lay.rep):
+        column = lax.dynamic_update_index_in_dim(column, lay.to_rep(shard, k), (z - k) % lay.rep, 0)
+    column = column.reshape(lay.rep * rows, cols)
+    plane = jnp.zeros((lay.plane, lay.rep * rows, cols), shard.dtype)
+    plane = lax.dynamic_update_index_in_dim(plane, column, p, 0)
+    for m in range(1, lay.plane):
+        plane = lax.dynamic_update_index_in_dim(plane, lay.to_plane(column, m), p ^ m, 0)
+    other = lay.to_core(plane)
+    first = jnp.where(c == 0, plane, other)
+    second = jnp.where(c == 0, other, plane)
+    return jnp.stack([first, second], axis=1).reshape(-1, cols)
+
+
+def scatter_rows(lay, total):
+    cols = total.shape[1]
+    p, c, z = lay.place()
+    split = total.reshape(lay.plane, 2, -1, cols)
+    sent = lay.to_core(pick(split, 1 - c, 1).astype(jnp.bfloat16))
+    chip = pick(split, c, 1) + sent.astype(jnp.float32)
+    low = chip.astype(jnp.bfloat16)
+    column = pick(chip, p, 0)
+    for m in range(1, lay.plane):
+        column = column + lay.to_plane(pick(low, p ^ m, 0), m).astype(jnp.float32)
+    column = column.reshape(lay.rep, -1, cols)
+    low = column.astype(jnp.bfloat16)
+    own = pick(column, z, 0)
+    for k in range(1, lay.rep):
+        own = own + lay.to_rep(pick(low, (z + k) % lay.rep, 0), k).astype(jnp.float32)
+    return own
+
+
+def sum_all(lay, row):
+    count = lay.dp * lay.rep
+    spread = jnp.broadcast_to(row[None, None, :], (count, 1, row.shape[0]))
+    return jnp.sum(lax.all_to_all(spread, AXES, 0, 0), axis=(0, 1))
 
 
 def body(
+    lay,
     inputs,
     segments,
     cotangent,
@@ -191,38 +270,29 @@
     masters = (attend_in, attend_out, expand, contract, layer_norms)
     local_weight_sums = jnp.stack([jnp.sum(weight * weight) for weight in masters])
     lowered = [weight.astype(jnp.bfloat16) for weight in masters]
+    norm_rows = jnp.pad(lowered[4].T, ((0, 0), (0, 124)))
+    first = gather_rows(lay, jnp.concatenate([lowered[0], norm_rows], axis=1))
+    second = gather_rows(lay, jnp.concatenate([lowered[1], lowered[2]], axis=1))
+    third = gather_rows(lay, lowered[3])
+    width = attend_in.shape[1]
     gathered = (
-        lax.all_gather(lowered[0], ("dp", "rep"), axis=0, tiled=True),
-        lax.all_gather(lowered[1], ("dp", "rep"), axis=0, tiled=True),
-        lax.all_gather(lowered[2], ("dp", "rep"), axis=0, tiled=True),
-        lax.all_gather(lowered[3], ("dp", "rep"), axis=0, tiled=True),
-        lax.all_gather(lowered[4], ("dp", "rep"), axis=1, tiled=True),
-    )
-
-    def forward_one(items):
-        return forward_sequence(gathered, items[0], items[1])[0].astype(jnp.bfloat16)
-
-    outputs = lax.map(forward_one, (inputs, segments))
-    regathered = (
-        lax.all_gather(lowered[0], ("dp", "rep"), axis=0, tiled=True),
-        lax.all_gather(lowered[1], ("dp", "rep"), axis=0, tiled=True),
-        lax.all_gather(lowered[2], ("dp", "rep"), axis=0, tiled=True),
-        lax.all_gather(lowered[3], ("dp", "rep"), axis=0, tiled=True),
-        lax.all_gather(lowered[4], ("dp", "rep"), axis=1, tiled=True),
-    )
-    zero_grads = tuple((jnp.zeros(weight.shape, jnp.float32) for weight in regathered))
-
-    def accumulate(carry, items):
-        grad_input, grads = backward_sequence(regathered, items[0], items[1], items[2])
-        return (tuple((total + piece for total, piece in zip(carry, grads))), grad_input)
-
-    summed, input_gradient = lax.scan(accumulate, zero_grads, (inputs, segments, cotangent))
+        first[:, :width],
+        second[:, : attend_out.shape[1]],
+        second[:, attend_out.shape[1] :],
+        third,
+        first[:, width : width + 4].T,
+    )
+    outputs, input_gradient, summed = backward_sequence(gathered, inputs[0], segments[0], cotangent[0])
+    outputs = outputs.astype(jnp.bfloat16)[None]
+    input_gradient = input_gradient[None]
+    last = scatter_rows(lay, jnp.concatenate([summed[0], jnp.pad(summed[4].T, ((0, 0), (0, 124)))], axis=1))
+    middle = scatter_rows(lay, jnp.concatenate([summed[1], summed[2]], axis=1))
     reduced = (
-        lax.psum_scatter(summed[0], ("dp", "rep"), scatter_dimension=0, tiled=True),
-        lax.psum_scatter(summed[1], ("dp", "rep"), scatter_dimension=0, tiled=True),
-        lax.psum_scatter(summed[2], ("dp", "rep"), scatter_dimension=0, tiled=True),
-        lax.psum_scatter(summed[3], ("dp", "rep"), scatter_dimension=0, tiled=True),
-        lax.psum_scatter(summed[4], ("dp", "rep"), scatter_dimension=1, tiled=True),
+        last[:, :width],
+        middle[:, : attend_out.shape[1]],
+        middle[:, attend_out.shape[1] :],
+        scatter_rows(lay, summed[3]),
+        last[:, width : width + 4].T,
     )
     firsts = (moment_in, moment_out, moment_expand, moment_contract, moment_norms)
     seconds = (square_in, square_out, square_expand, square_contract, square_norms)
@@ -236,7 +306,8 @@
         variances.append(variance)
         directions.append(momentum / (jnp.sqrt(variance) + ADAM_EPSILON) + DECAY * weight)
     local_update_sums = jnp.stack([jnp.sum(direction * direction) for direction in directions])
-    weight_sums, update_sums = lax.psum((local_weight_sums, local_update_sums), ("dp", "rep"))
+    sums = sum_all(lay, jnp.pad(jnp.concatenate([local_weight_sums, local_update_sums]), (0, 118)))
+    weight_sums, update_sums = sums[:5], sums[5:10]
     weight_norms = jnp.sqrt(weight_sums)
     update_norms = jnp.sqrt(update_sums)
     ratios = weight_norms / update_norms
@@ -289,7 +360,7 @@
         P(None, ("dp", "rep")),
     )
     return jax.shard_map(
-        body,
+        partial(body, Layout(mesh)),
         mesh=mesh,
         in_specs=placed,
         out_specs=(

time: 1180 us -> 450 us (0.38)
  waiting for transfers between devices: 642 us -> 49.4 us
  blocking collectives: 181 us -> 0 us
  starting transfers between devices: 0.5 us -> 80.2 us
  matrix products: 218 us -> 163 us
  local copies, waits for them, and re-layouts: 48.7 us -> 84 us
  between operations: 18.3 us -> 5.02 us
    reduce_scatter x4 -> x0, waiting for transfers between devices: 526 us -> none  [the longest x1 147 us: body(): lax.psum_scatter(summed[2], ('dp', 'rep'), scatter_dimension=0, tiled=True)]
    all_gather x2 -> x0, blocking collectives: 144 us -> none  [the longest x1 73.8 us: body(): lax.all_gather(lowered[1], ('dp', 'rep'), axis=0, tiled=True)]
    ppermute x0 -> x42, starting transfers between devices: none -> 75.8 us  [permute(): return lax.ppermute(value, AXES, pairs)]
    unnamed x9 -> x0, waiting for transfers between devices: 60 us -> none
    all_gather x3 -> x0, waiting for transfers between devices: 55.8 us -> none  [the longest x1 55.7 us: body(): lax.all_gather(lowered[3], ('dp', 'rep'), axis=0, tiled=True)]
    ppermute x0 -> x42, waiting for transfers between devices: none -> 49.4 us  [permute(): return lax.ppermute(value, AXES, pairs)]
    psum x1 -> x0, blocking collectives: 37.5 us -> none  [body(): lax.psum((local_weight_sums, local_update_sums), ('dp', 'rep'))]
    dot_general x24 -> x16, matrix products: 67 us -> 46.3 us  [head_scores(): jnp.einsum('qd,kd->qk', queries, keys, preferred_element_type=jnp.float32)]
  transfers between devices with their start and end apart: 8 -> 43, of which waited for: 6 -> 13; matrix products, arithmetic and copies ran while one was open for 13% -> 26% of each run, Pallas kernels for 0% -> 0%
where the time goes in v1:
time: 450 us; the launch traced here: 442 us
  matrix products  163 us (36%)
  local copies, waits for them, and re-layouts  84 us (19%)
  starting transfers between devices  80.2 us (18%)
  other arithmetic  59.9 us (13%)
  waiting for transfers between devices  49.4 us (11%)
  between operations  5.02 us (1%)
    ppermute x42, starting transfers between devices, permute(): return lax.ppermute(value, AXES, pairs)  75.8 us
    ppermute x42, waiting for transfers between devices, permute(): return lax.ppermute(value, AXES, pairs)  49.4 us
    dot_general x16, matrix products, head_scores(): jnp.einsum('qd,kd->qk', queries, keys, preferred_element_type=jnp.float32)  46.3 us
    unnamed x114, local copies, waits for them, and re-layouts  21.4 us
    dot_general x8, matrix products, head_back(): jnp.einsum('qd,kd->qk', upstream, values, preferred_element_type=jnp.floa...  14.9 us
    dot_general x8, matrix products, head_back(): jnp.einsum('qk,qd->kd', attention.astype(jnp.bfloat16), upstream, preferr...  14.6 us
    dot_general x8, matrix products, head_back(): jnp.einsum('qk,qd->kd', grad_scores, queries, preferred_element_type=jnp....  14.3 us
    dot_general x8, matrix products, one_head(): jnp.dot(attention, values, preferred_element_type=jnp.float32)  13.2 us
  transfers between devices with their start and end apart: 43, of which 13 were waited for; matrix products, arithmetic and copies ran while one was open for 26% of the time, Pallas kernels for 0%

profile of v1, /device:TPU:0, one launch (start us, length us, event | category | flops | bytes accessed | tf_op | source)
XLA Modules:
  0.0 442.1 jit_solution(8841778046041528138)
XLA Ops:
  2.5 4.1 collective-permute-start.8
  21.3 3.3 collective-permute-start.2
  28.5 5.3 %collective-permute-done.14 = bf16[64,512]{1,0:T(8,128)(2,1)S(1)} collective-permute-done((bf16[64,512]{1,0:T(8,128)(2,1)S(1)}, bf16[64,512]{1,0:T(8,128)(2,1)S(1)}, u32[]{:S(2)}, u32[]{:S(2)}) %collective-permute-start.14) | collective-permute-done | bytes 65568 | tf_op jit(solution)/shard_map/ppermute | solution.py:187
  54.4 6.5 %collective-permute-done.17 = bf16[256,512]{1,0:T(8,128)(2,1)S(1)} collective-permute-done((bf16[256,512]{1,0:T(8,128)(2,1)S(1)}, bf16[256,512]{1,0:T(8,128)(2,1)S(1)}, u32[]{:S(2)}, u32[]{:S(2)}) %collective-permute-start.17) | collective-permute-done | bytes 262176 | tf_op jit(solution)/shard_map/ppermute | solution.py:187
  66.0 5.4 %collective-permute-done.10 = bf16[64,2560]{1,0:T(8,128)(2,1)S(1)} collective-permute-done((bf16[64,2560]{1,0:T(8,128)(2,1)S(1)}, bf16[64,2560]{1,0:T(8,128)(2,1)S(1)}, u32[]{:S(2)}, u32[]{:S(2)}) %collective-permute-start.10) | collective-permute-done | bytes 327712 | tf_op jit(solution)/shard_map/ppermute | solution.py:187
  75.2 3.7 convolution_convert_fusion
  78.8 4.4 copy.183
  88.0 3.8 copy.185
  94.1 44.5 %while.24 = (s32[]{:T(128)}, bf16[8,1044,64]{1,2,0:T(8,128)(2,1)}, f32[8,1044,1]{1,2,0:T(1,128)}, bf16[8,1044,64]{2,1,0:T(8,128)(2,1)}, bf16[8,1044,64]{2,1,0:T(...) while((s32[]{:T(128)}, bf16[8,1044,64]{1,2,0:T(8,128)(2,1)}, ...), condition=%wide.region_5.6_spmd.clone, body=%wide.region_2.5_spmd.clone.sunk | while | flops 291011872 | bytes 14721305 | solution.py:72
  146.1 5.6 %fusion.62 = (bf16[2048,1044]{0,1:T(8,128)(2,1)}, f32[1044,2048]{1,0:T(8,128)S(1)}) fusion(bf16[512,2560]{1,0:T(8,128)(2,1)S(1)} %bitcast.394, f32[1044,512]{1,0:T(8,128)S(1)} %get-tuple-element.489, f32[512]{0:T(512)S(1)} %get-tuple-element.380, f32[512]{0:T(512)S(1)} %get-tuple-element.379, f32[1044]{0:T(1024)S(1)} %add_rsqrt_fusion, ...), kind=kOutput, calls=%fused_computation.74 | convolution fusion | flops 2211342336 | bytes 17092608 | tf_op jit(solution)/shard_map/dot_general | solution.py:77
  151.7 3.9 fusion.68
  155.7 7.8 %fusion.54 = bf16[1044,2048]{1,0:T(8,128)(2,1)S(1)} fusion(f32[1044,2048]{1,0:T(8,128)S(1)} %get-tuple-element.492, bf16[2048,512]{1,0:T(8,128)(2,1)S(1)} %bitcast.406, bf16[1,1044,512]{2,1,0:T(8,128)(2,1)S(1)} %copy-done.21), kind=kOutput, calls=%fused_computation.66 | convolution fusion | flops 2232188928 | bytes 15994880 | tf_op jit(solution)/shard_map/rd,fd->rf/dot_general | solution.py:120
  166.5 5.2 %fusion.143 = f32[512,2048]{1,0:T(8,128)} fusion(bf16[1044,2048]{1,0:T(8,128)(2,1)S(1)} %fusion.54, f32[1044,512]{1,0:T(8,128)S(1)} %get-tuple-element.489, f32[512]{0:T(512)S(1)} %get-tuple-element.380, f32[512]{0:T(512)S(1)} %get-tuple-element.379, f32[1044]{0:T(1024)S(1)} %add_rsqrt_fusion, f32[1044]{0:T(1024)S(1)} %broadcast_multiply_fusion.7), kind=kOutput, calls=%fused_computation.294 | convolution fusion | flops 2192099328 | bytes 10621088 | tf_op jit(solution)/shard_map/rd,rf->df/dot_general | solution.py:123
  178.7 99.9 %while.25 = (s32[]{:T(128)}, bf16[8,3,1044,64]{2,3,1,0:T(8,128)(2,1)}, bf16[8,1044,64]{2,1,0:T(8,128)(2,1)}, bf16[8,1044,64]{2,1,0:T(8,128)(2,1)}, f32[8,1044,1]...) while((s32[]{:T(128)}, ...), condition=%wide.region_12.13_spmd.clone, body=%wide.region_10.12_spmd.clone.sunk | while | flops 712107200 | bytes 36095584 | solution.py:159
  181.3 3.2 multiply_reduce_fusion.17
  193.7 3.2 multiply_reduce_fusion.17
  218.6 3.2 multiply_reduce_fusion.17
  243.5 3.2 multiply_reduce_fusion.17
  268.3 3.2 multiply_reduce_fusion.17
  281.1 4.1 fusion.83
  285.2 4.4 fusion.98
  289.6 10.7 %dot_general.76 = bf16[4,2,256,1044]{2,1,0,3:T(2,128)(2,1)} reshape(bf16[2048,1044]{0,1:T(8,128)(2,1)} %get-tuple-element.491) | data formatting | bytes 8552448 | tf_op jit(solution)/shard_map/rf,rd->fd/dot_general | solution.py:119
  300.3 5.3 %fusion.63 = f32[4,2,256,512]{3,2,1,0:T(8,128)S(1)} fusion(bf16[4,2,256,1044]{2,1,0,3:T(2,128)(2,1)} %dot_general.76, bf16[1,1044,512]{2,1,0:T(8,128)(2,1)} %param.24), kind=kOutput, calls=%fused_computation.78 | convolution fusion | flops 2189426688 | bytes 9539584 | tf_op jit(solution)/shard_map/rf,rd->fd/dot_general | solution.py:119
  325.8 4.3 collective-permute-done.24
  339.3 18.0 %collective-permute-done.26 = bf16[16,1664]{0,1:T(8,128)(2,1)} collective-permute-done((bf16[16,1664]{0,1:T(8,128)(2,1)}, bf16[16,1664]{0,1:T(8,128)(2,1)}, u32[]{:S(2)}, u32[]{:S(2)}) %collective-permute-start.26) | collective-permute-done | bytes 53280 | tf_op jit(solution)/shard_map/ppermute | solution.py:187
  358.9 6.5 %collective-permute-start.37 = (bf16[256,512]{1,0:T(8,128)(2,1)}, bf16[256,512]{1,0:T(8,128)(2,1)S(1)}, u32[]{:S(2)}, u32[]{:S(2)}) collective-permute-start(bf16[256,512]{1,0:T(8,128)(2,1)} %get-tuple-element.463), channel_id=1, source_target_pairs={{0,16},{1,17},{2,18},{3,19},{4,20},{5,21},{6,22},{7,23},{8,24},{9,... | collective-permute-start | bytes 786440 | tf_op jit(solution)/shard_map/ppermute | solution.py:187
  379.6 10.7 %collective-permute-start.39 = (bf16[64,512]{1,0:T(8,128)(2,1)S(1)}, bf16[64,512]{1,0:T(8,128)(2,1)S(1)}, u32[]{:S(2)}, u32[]{:S(2)}) collective-permute-start(bf16[64,512]{1,0:T(8,128)(2,1)S(1)} %get-tuple-element.470), channel_id=1, source_target_pairs={{0,1},{1,2},{2,3},{3,0},{4,5},{5,6},{6,7},{7,4},{8,9},{9,10},{10,1... | collective-permute-start | bytes 196616 | tf_op jit(solution)/shard_map/ppermute | solution.py:187
  390.3 6.0 %collective-permute-start.40 = (bf16[64,512]{1,0:T(8,128)(2,1)S(1)}, bf16[64,512]{1,0:T(8,128)(2,1)S(1)}, u32[]{:S(2)}, u32[]{:S(2)}) collective-permute-start(bf16[64,512]{1,0:T(8,128)(2,1)S(1)} %get-tuple-element.472), channel_id=1, source_target_pairs={{0,2},{1,3},{2,0},{3,1},{4,6},{5,7},{6,4},{7,5},{8,10},{9,11},{10,... | collective-permute-start | bytes 196616 | tf_op jit(solution)/shard_map/ppermute | solution.py:187
  396.6 7.8 %collective-permute-start.32 = (bf16[16,2560]{1,0:T(8,128)(2,1)S(1)}, bf16[16,2560]{1,0:T(8,128)(2,1)S(1)}, u32[]{:S(2)}, u32[]{:S(2)}) collective-permute-start(bf16[16,2560]{1,0:T(8,128)(2,1)S(1)} %get-tuple-element.467), channel_id=1, source_target_pairs={{0,1},{1,2},{2,3},{3,0},{4,5},{5,6},{6,7},{7,4},{8,9},{9,10},{10,1... | collective-permute-start | bytes 245768 | tf_op jit(solution)/shard_map/ppermute | solution.py:187
  412.9 6.9 %concatenate.23 = f32[10]{0:T(128)} concatenate(f32[1]{0:T(128)} %bitcast.59, f32[1]{0:T(128)} %bitcast.60, f32[1]{0:T(128)} %bitcast.61, f32[1]{0:T(128)} %bitcast.62, f32[1]{0:T(128)} %bitcast.63, f32[1]{0:T(128)} %bitcast.82, f32[1]{0:T(128)} %bitcast.96, f32[1]{0:T(128)} %bitcast.97, f32[1]{0:T(128)} %bitcast.112, f32[1]{0:T(128)} %bitcast.114), dimensions={0} | concatenate | bytes 80 | tf_op jit(solution)/shard_map/concatenate | solution.py:309
  421.0 4.4 all-to-all-start
  425.4 3.3 fusion.100
  (403 shorter events, 269.1 us)
Async XLA Ops:
  2.5 40.5 %collective-permute-start.8 = (bf16[16,2560]{1,0:T(8,128)(2,1)S(1)}, bf16[16,2560]{1,0:T(8,128)(2,1)S(1)}, u32[]{:S(2)}, u32[]{:S(2)}) collective-permute-start(bf16[16,2560]{1,0:T(8,128)(2,1)S(1)} %pad_maximum_fusion.4), channel_id=1, source_target_pairs={{0,2},{1,3},{2,0},{3,1},{4,6},{5,7},{6,4},{7,5},{8,10},{9,11},{10,... | collective-permute-start | bytes 245768 | tf_op jit(solution)/shard_map/ppermute | solution.py:187
  6.6 34.9 %collective-permute-start.7 = (bf16[16,2560]{1,0:T(8,128)(2,1)S(1)}, bf16[16,2560]{1,0:T(8,128)(2,1)S(1)}, u32[]{:S(2)}, u32[]{:S(2)}) collective-permute-start(bf16[16,2560]{1,0:T(8,128)(2,1)S(1)} %pad_maximum_fusion.4), channel_id=1, source_target_pairs={{0,1},{1,2},{2,3},{3,0},{4,5},{5,6},{6,7},{7,4},{8,9},{9,10},{10,1... | collective-permute-start | bytes 245768 | tf_op jit(solution)/shard_map/ppermute | solution.py:187
  8.2 35.4 %collective-permute-start.9 = (bf16[16,2560]{1,0:T(8,128)(2,1)S(1)}, bf16[16,2560]{1,0:T(8,128)(2,1)S(1)}, u32[]{:S(2)}, u32[]{:S(2)}) collective-permute-start(bf16[16,2560]{1,0:T(8,128)(2,1)S(1)} %pad_maximum_fusion.4), channel_id=1, source_target_pairs={{0,3},{1,0},{2,1},{3,2},{4,7},{5,4},{6,5},{7,6},{8,11},{9,8},{10,9... | collective-permute-start | bytes 245768 | tf_op jit(solution)/shard_map/ppermute | solution.py:187
  12.8 11.8 %collective-permute-start.1 = (bf16[16,1664]{1,0:T(8,128)(2,1)S(1)}, bf16[16,1664]{1,0:T(8,128)(2,1)S(1)}, u32[]{:S(2)}, u32[]{:S(2)}) collective-permute-start(bf16[16,1664]{1,0:T(8,128)(2,1)S(1)} %fusion.133), channel_id=1, source_target_pairs={{0,2},{1,3},{2,0},{3,1},{4,6},{5,7},{6,4},{7,5},{8,10},{9,11},{10,... | collective-permute-start | bytes 159752 | tf_op jit(solution)/shard_map/ppermute | solution.py:187
  24.6 10.8 %collective-permute-start.15 = (bf16[64,512]{1,0:T(8,128)(2,1)S(1)}, bf16[64,512]{1,0:T(8,128)(2,1)S(1)}, u32[]{:S(2)}, u32[]{:S(2)}) collective-permute-start(bf16[64,512]{1,0:T(8,128)(2,1)S(1)} %get-tuple-element.444), channel_id=1, source_target_pairs={{0,2},{1,3},{2,0},{3,1},{4,6},{5,7},{6,4},{7,5},{8,10},{9,11},{10,... | collective-permute-start | bytes 196616 | tf_op jit(solution)/shard_map/ppermute | solution.py:187
  35.4 18.4 %collective-permute-start.5 = (bf16[64,1664]{1,0:T(8,128)(2,1)S(1)}, bf16[64,1664]{1,0:T(8,128)(2,1)S(1)}, u32[]{:S(2)}, u32[]{:S(2)}) collective-permute-start(bf16[64,1664]{1,0:T(8,128)(2,1)S(1)} %bitcast.422), channel_id=1, source_target_pairs={{0,24},{1,25},{2,26},{3,27},{4,28},{5,29},{6,30},{7,31},{8,16},{9,... | collective-permute-start | bytes 638984 | tf_op jit(solution)/shard_map/ppermute | solution.py:187
  38.1 13.2 %collective-permute-start.4 = (bf16[64,1664]{1,0:T(8,128)(2,1)S(1)}, bf16[64,1664]{1,0:T(8,128)(2,1)S(1)}, u32[]{:S(2)}, u32[]{:S(2)}) collective-permute-start(bf16[64,1664]{1,0:T(8,128)(2,1)S(1)} %bitcast.423), channel_id=1, source_target_pairs={{0,16},{1,17},{2,18},{3,19},{4,20},{5,21},{6,22},{7,23},{8,24},{9,... | collective-permute-start | bytes 638984 | tf_op jit(solution)/shard_map/ppermute | solution.py:187
  43.0 21.8 %collective-permute-start.19 = (bf16[256,512]{1,0:T(8,128)(2,1)S(1)}, bf16[256,512]{1,0:T(8,128)(2,1)S(1)}, u32[]{:S(2)}, u32[]{:S(2)}) collective-permute-start(bf16[256,512]{1,0:T(8,128)(2,1)S(1)} %bitcast.417), channel_id=1, source_target_pairs={{0,24},{1,25},{2,26},{3,27},{4,28},{5,29},{6,30},{7,31},{8,16},{9,... | collective-permute-start | bytes 786440 | tf_op jit(solution)/shard_map/ppermute | solution.py:187
  43.5 20.5 %collective-permute-start.18 = (bf16[256,512]{1,0:T(8,128)(2,1)S(1)}, bf16[256,512]{1,0:T(8,128)(2,1)S(1)}, u32[]{:S(2)}, u32[]{:S(2)}) collective-permute-start(bf16[256,512]{1,0:T(8,128)(2,1)S(1)} %bitcast.418), channel_id=1, source_target_pairs={{0,16},{1,17},{2,18},{3,19},{4,20},{5,21},{6,22},{7,23},{8,24},{9,... | collective-permute-start | bytes 786440 | tf_op jit(solution)/shard_map/ppermute | solution.py:187
  49.6 11.3 %collective-permute-start.17 = (bf16[256,512]{1,0:T(8,128)(2,1)S(1)}, bf16[256,512]{1,0:T(8,128)(2,1)S(1)}, u32[]{:S(2)}, u32[]{:S(2)}) collective-permute-start(bf16[256,512]{1,0:T(8,128)(2,1)S(1)} %bitcast.419), channel_id=1, source_target_pairs={{0,8},{1,9},{2,10},{3,11},{4,12},{5,13},{6,14},{7,15},{8,0},{9,1},... | collective-permute-start | bytes 786440 | tf_op jit(solution)/shard_map/ppermute | solution.py:187
  51.4 21.5 %collective-permute-start.12 = (bf16[64,2560]{1,0:T(8,128)(2,1)S(1)}, bf16[64,2560]{1,0:T(8,128)(2,1)S(1)}, u32[]{:S(2)}, u32[]{:S(2)}) collective-permute-start(bf16[64,2560]{1,0:T(8,128)(2,1)S(1)} %bitcast.411), channel_id=1, source_target_pairs={{0,24},{1,25},{2,26},{3,27},{4,28},{5,29},{6,30},{7,31},{8,16},{9,... | collective-permute-start | bytes 983048 | tf_op jit(solution)/shard_map/ppermute | solution.py:187
  53.8 18.3 %collective-permute-start.11 = (bf16[64,2560]{1,0:T(8,128)(2,1)S(1)}, bf16[64,2560]{1,0:T(8,128)(2,1)S(1)}, u32[]{:S(2)}, u32[]{:S(2)}) collective-permute-start(bf16[64,2560]{1,0:T(8,128)(2,1)S(1)} %bitcast.412), channel_id=1, source_target_pairs={{0,16},{1,17},{2,18},{3,19},{4,20},{5,21},{6,22},{7,23},{8,24},{9,... | collective-permute-start | bytes 983048 | tf_op jit(solution)/shard_map/ppermute | solution.py:187
  65.5 73.1 %collective-permute-start.20 = (bf16[4,256,512]{2,1,0:T(8,128)(2,1)}, bf16[4,256,512]{2,1,0:T(8,128)(2,1)}, u32[]{:S(2)}, u32[]{:S(2)}) collective-permute-start(bf16[4,256,512]{2,1,0:T(8,128)(2,1)} %bitcast_dynamic-update-slice_fusion.4), channel_id=1, source_target_pairs={{0,4},{1,5},{2,6},{3,7},{4,0},{5,1},{6,2},{7,3},{8,12},{9,13},{10,... | collective-permute-start | bytes 3145736 | tf_op jit(solution)/shard_map/ppermute | solution.py:187
  73.6 67.7 %collective-permute-start.13 = (bf16[4,64,2560]{2,1,0:T(8,128)(2,1)}, bf16[4,64,2560]{2,1,0:T(8,128)(2,1)}, u32[]{:S(2)}, u32[]{:S(2)}) collective-permute-start(bf16[4,64,2560]{2,1,0:T(8,128)(2,1)} %bitcast_dynamic-update-slice_fusion), channel_id=1, source_target_pairs={{0,4},{1,5},{2,6},{3,7},{4,0},{5,1},{6,2},{7,3},{8,12},{9,13},{10,... | collective-permute-start | bytes 3932168 | tf_op jit(solution)/shard_map/ppermute | solution.py:187
  308.6 11.9 %collective-permute-start.35 = (bf16[4,256,512]{2,1,0:T(8,128)(2,1)}, bf16[4,256,512]{2,1,0:T(8,128)(2,1)}, u32[]{:S(2)}, u32[]{:S(2)}) collective-permute-start(bf16[4,256,512]{2,1,0:T(8,128)(2,1)} %fusion.112), channel_id=1, source_target_pairs={{0,4},{1,5},{2,6},{3,7},{4,0},{5,1},{6,2},{7,3},{8,12},{9,13},{10,... | collective-permute-start | bytes 3145736 | tf_op jit(solution)/shard_map/ppermute | solution.py:187
  316.0 57.3 %collective-permute-start.28 = (bf16[4,64,2560]{2,1,0:T(8,128)(2,1)}, bf16[4,64,2560]{2,1,0:T(8,128)(2,1)}, u32[]{:S(2)}, u32[]{:S(2)}) collective-permute-start(bf16[4,64,2560]{2,1,0:T(8,128)(2,1)} %fusion.96), channel_id=1, source_target_pairs={{0,4},{1,5},{2,6},{3,7},{4,0},{5,1},{6,2},{7,3},{8,12},{9,13},{10,... | collective-permute-start | bytes 3932168 | tf_op jit(solution)/shard_map/ppermute | solution.py:187
  318.4 11.6 %collective-permute-start.24 = (bf16[64,1664]{1,0:T(8,128)(2,1)S(1)}, bf16[64,1664]{1,0:T(8,128)(2,1)S(1)}, u32[]{:S(2)}, u32[]{:S(2)}) collective-permute-start(bf16[64,1664]{1,0:T(8,128)(2,1)S(1)} %get-tuple-element.465), channel_id=1, source_target_pairs={{0,24},{1,25},{2,26},{3,27},{4,28},{5,29},{6,30},{7,31},{8,16},{9,... | collective-permute-start | bytes 638984 | tf_op jit(solution)/shard_map/ppermute | solution.py:187
  319.5 11.7 %collective-permute-start.23 = (bf16[64,1664]{1,0:T(8,128)(2,1)S(1)}, bf16[64,1664]{1,0:T(8,128)(2,1)S(1)}, u32[]{:S(2)}, u32[]{:S(2)}) collective-permute-start(bf16[64,1664]{1,0:T(8,128)(2,1)S(1)} %get-tuple-element.466), channel_id=1, source_target_pairs={{0,16},{1,17},{2,18},{3,19},{4,20},{5,21},{6,22},{7,23},{8,24},{9,... | collective-permute-start | bytes 638984 | tf_op jit(solution)/shard_map/ppermute | solution.py:187
  324.3 46.5 %collective-permute-start.36 = (bf16[256,512]{1,0:T(8,128)(2,1)}, bf16[256,512]{1,0:T(8,128)(2,1)}, u32[]{:S(2)}, u32[]{:S(2)}) collective-permute-start(bf16[256,512]{1,0:T(8,128)(2,1)} %get-tuple-element.461), channel_id=1, source_target_pairs={{0,8},{1,9},{2,10},{3,11},{4,12},{5,13},{6,14},{7,15},{8,0},{9,1},... | collective-permute-start | bytes 786440 | tf_op jit(solution)/shard_map/ppermute | solution.py:187
  335.0 22.3 %collective-permute-start.26 = (bf16[16,1664]{0,1:T(8,128)(2,1)}, bf16[16,1664]{0,1:T(8,128)(2,1)}, u32[]{:S(2)}, u32[]{:S(2)}) collective-permute-start(bf16[16,1664]{0,1:T(8,128)(2,1)} %copy.199), channel_id=1, source_target_pairs={{0,2},{1,3},{2,0},{3,1},{4,6},{5,7},{6,4},{7,5},{8,10},{9,11},{10,... | collective-permute-start | bytes 159752 | tf_op jit(solution)/shard_map/ppermute | solution.py:187
  335.0 23.9 %collective-permute-start.27 = (bf16[16,1664]{0,1:T(8,128)(2,1)}, bf16[16,1664]{0,1:T(8,128)(2,1)}, u32[]{:S(2)}, u32[]{:S(2)}) collective-permute-start(bf16[16,1664]{0,1:T(8,128)(2,1)} %copy.200), channel_id=1, source_target_pairs={{0,3},{1,0},{2,1},{3,2},{4,7},{5,4},{6,5},{7,6},{8,11},{9,8},{10,9... | collective-permute-start | bytes 159752 | tf_op jit(solution)/shard_map/ppermute | solution.py:187
  337.0 28.4 %collective-permute-start.25 = (bf16[16,1664]{0,1:T(8,128)(2,1)}, bf16[16,1664]{0,1:T(8,128)(2,1)}, u32[]{:S(2)}, u32[]{:S(2)}) collective-permute-start(bf16[16,1664]{0,1:T(8,128)(2,1)} %copy.197), channel_id=1, source_target_pairs={{0,1},{1,2},{2,3},{3,0},{4,5},{5,6},{6,7},{7,4},{8,9},{9,10},{10,1... | collective-permute-start | bytes 159752 | tf_op jit(solution)/shard_map/ppermute | solution.py:187
  357.3 13.5 %collective-permute-start.38 = (bf16[256,512]{1,0:T(8,128)(2,1)}, bf16[256,512]{1,0:T(8,128)(2,1)S(1)}, u32[]{:S(2)}, u32[]{:S(2)}) collective-permute-start(bf16[256,512]{1,0:T(8,128)(2,1)} %get-tuple-element.462), channel_id=1, source_target_pairs={{0,24},{1,25},{2,26},{3,27},{4,28},{5,29},{6,30},{7,31},{8,16},{9,... | collective-permute-start | bytes 786440 | tf_op jit(solution)/shard_map/ppermute | solution.py:187
  358.9 13.1 %collective-permute-start.37 = (bf16[256,512]{1,0:T(8,128)(2,1)}, bf16[256,512]{1,0:T(8,128)(2,1)S(1)}, u32[]{:S(2)}, u32[]{:S(2)}) collective-permute-start(bf16[256,512]{1,0:T(8,128)(2,1)} %get-tuple-element.463), channel_id=1, source_target_pairs={{0,16},{1,17},{2,18},{3,19},{4,20},{5,21},{6,22},{7,23},{8,24},{9,... | collective-permute-start | bytes 786440 | tf_op jit(solution)/shard_map/ppermute | solution.py:187
  376.0 14.3 %collective-permute-start.29 = (bf16[64,2560]{1,0:T(8,128)(2,1)S(1)}, bf16[64,2560]{1,0:T(8,128)(2,1)S(1)}, u32[]{:S(2)}, u32[]{:S(2)}) collective-permute-start(bf16[64,2560]{1,0:T(8,128)(2,1)S(1)} %get-tuple-element.458), channel_id=1, source_target_pairs={{0,8},{1,9},{2,10},{3,11},{4,12},{5,13},{6,14},{7,15},{8,0},{9,1},... | collective-permute-start | bytes 983048 | tf_op jit(solution)/shard_map/ppermute | solution.py:187
  376.7 19.6 %collective-permute-start.31 = (bf16[64,2560]{1,0:T(8,128)(2,1)S(1)}, bf16[64,2560]{1,0:T(8,128)(2,1)S(1)}, u32[]{:S(2)}, u32[]{:S(2)}) collective-permute-start(bf16[64,2560]{1,0:T(8,128)(2,1)S(1)} %get-tuple-element.459), channel_id=1, source_target_pairs={{0,24},{1,25},{2,26},{3,27},{4,28},{5,29},{6,30},{7,31},{8,16},{9,... | collective-permute-start | bytes 983048 | tf_op jit(solution)/shard_map/ppermute | solution.py:187
  378.2 18.0 %collective-permute-start.30 = (bf16[64,2560]{1,0:T(8,128)(2,1)S(1)}, bf16[64,2560]{1,0:T(8,128)(2,1)S(1)}, u32[]{:S(2)}, u32[]{:S(2)}) collective-permute-start(bf16[64,2560]{1,0:T(8,128)(2,1)S(1)} %get-tuple-element.460), channel_id=1, source_target_pairs={{0,16},{1,17},{2,18},{3,19},{4,20},{5,21},{6,22},{7,23},{8,24},{9,... | collective-permute-start | bytes 983048 | tf_op jit(solution)/shard_map/ppermute | solution.py:187
  379.6 24.9 %collective-permute-start.39 = (bf16[64,512]{1,0:T(8,128)(2,1)S(1)}, bf16[64,512]{1,0:T(8,128)(2,1)S(1)}, u32[]{:S(2)}, u32[]{:S(2)}) collective-permute-start(bf16[64,512]{1,0:T(8,128)(2,1)S(1)} %get-tuple-element.470), channel_id=1, source_target_pairs={{0,1},{1,2},{2,3},{3,0},{4,5},{5,6},{6,7},{7,4},{8,9},{9,10},{10,1... | collective-permute-start | bytes 196616 | tf_op jit(solution)/shard_map/ppermute | solution.py:187
  390.3 15.6 %collective-permute-start.41 = (bf16[64,512]{1,0:T(8,128)(2,1)S(1)}, bf16[64,512]{1,0:T(8,128)(2,1)S(1)}, u32[]{:S(2)}, u32[]{:S(2)}) collective-permute-start(bf16[64,512]{1,0:T(8,128)(2,1)S(1)} %get-tuple-element.471), channel_id=1, source_target_pairs={{0,3},{1,0},{2,1},{3,2},{4,7},{5,4},{6,5},{7,6},{8,11},{9,8},{10,9... | collective-permute-start | bytes 196616 | tf_op jit(solution)/shard_map/ppermute | solution.py:187
  390.3 15.6 %collective-permute-start.40 = (bf16[64,512]{1,0:T(8,128)(2,1)S(1)}, bf16[64,512]{1,0:T(8,128)(2,1)S(1)}, u32[]{:S(2)}, u32[]{:S(2)}) collective-permute-start(bf16[64,512]{1,0:T(8,128)(2,1)S(1)} %get-tuple-element.472), channel_id=1, source_target_pairs={{0,2},{1,3},{2,0},{3,1},{4,6},{5,7},{6,4},{7,5},{8,10},{9,11},{10,... | collective-permute-start | bytes 196616 | tf_op jit(solution)/shard_map/ppermute | solution.py:187
  396.6 10.9 %collective-permute-start.32 = (bf16[16,2560]{1,0:T(8,128)(2,1)S(1)}, bf16[16,2560]{1,0:T(8,128)(2,1)S(1)}, u32[]{:S(2)}, u32[]{:S(2)}) collective-permute-start(bf16[16,2560]{1,0:T(8,128)(2,1)S(1)} %get-tuple-element.467), channel_id=1, source_target_pairs={{0,1},{1,2},{2,3},{3,0},{4,5},{5,6},{6,7},{7,4},{8,9},{9,10},{10,1... | collective-permute-start | bytes 245768 | tf_op jit(solution)/shard_map/ppermute | solution.py:187
  421.0 11.9 %all-to-all-start = ((f32[32,1,128]{2,1,0:T(1,128)}), f32[32,1,128]{2,1,0:T(1,128)}, u32[]{:S(2)}, u32[]{:S(2)}) async-start(f32[32,1,128]{2,1,0:T(1,128)} %broadcast_in_dim.184), calls=%async_computation | async-start | bytes 32768 | tf_op jit(solution)/shard_map/all_to_all | solution.py:246
  (64 other events, 672.2 us)
